TPU v7x, 256 devices: a whole 4x4x8 slice. The times are simulated.
256 devices in a mesh: section: 8 (over y, core), row: 32 (over z, x).
Axes of the slice: x: 4, y: 4, z: 8, core: 2. Of those that a mesh axis runs over, the one named last changes fastest.
Arguments:
- channel_rows_in: bfloat16 [1024, 32, 4096], P('row', None, 'section'), may hold values from -6 to 6
- gate_rows_in: bfloat16 [1024, 32, 4096], P('row', None, 'section'), may hold values from -6 to 6
- map_input_rows: bfloat16 [1024, 32, 256], P('row'), may hold values from -6 to 6
- step_size_input: bfloat16 [1024, 64, 32], P('row', 'section'), may hold values from -4 to 4
- channel_kernel_weight: float32 [4, 4096], P(None, 'section'), may hold values from -3 to 3
- map_kernel_weight: float32 [4, 256], replicated, may hold values from -3 to 3
- channel_conv_bias: float32 [4096], P('section'), may hold values from -3 to 3
- map_kernel_bias: float32 [256], replicated, may hold values from -3 to 3
- step_size_bias: float32 [64], P('section'), may hold values from -2 to 0
- head_decay_rate: float32 [64], P('section'), may hold values from 0.003 to 1
- head_skip_weight: float32 [64], P('section'), may hold values from 0.5 to 1.5
- gated_norm_scale: float32 [4096], P('section'), may hold values from 0.5 to 1.5
- scan_state_cache: bfloat16 [1024, 64, 64, 128], P('row', 'section'), may hold values from -2 to 2
- channel_window_cache: bfloat16 [1024, 3, 4096], P('row', None, 'section'), may hold values from -6 to 6
- map_window_cache: bfloat16 [1024, 3, 256], P('row'), may hold values from -6 to 6
- adapter_down_weight: bfloat16 [32, 64, 4096], P('row', None, 'section'), may hold values from -0.09375 to 0.09375
- adapter_up_weight: bfloat16 [32, 64, 4096], P('row', None, 'section'), may hold values from -0.75 to 0.75
- session_slot_index: int32 [1024], replicated, may hold values from 0 to 1023, as said below
- lengths: int32 [1024], replicated, may hold values from 1 to 32
- session_adapter_index: int32 [1024], replicated, may hold values from 0 to 31
Outputs:
- mixer_output_rows: bfloat16 [1024, 32, 4096], P('row', None, 'section')
- adapter_delta: bfloat16 [1024, 32, 4096], P('row', None, 'section')
- scan_state_next: bfloat16 [1024, 64, 64, 128], P('row', 'section')
- channel_window_next: bfloat16 [1024, 3, 4096], P('row', None, 'section')
- map_window_next: bfloat16 [1024, 3, 256], P('row')
Inputs may be any that keep to these rules, and one draw needn't show every extreme that they name: `session_slot_index`: A permutation of the 1024 cache slots; cache slot c lies on row c // 32 and served session q on row q // 32. The states of one serving row's sessions come from exactly 16 home rows, 2 from each, so every home row also sends to that many rows.
All inputs are finite; a program needn't handle non-finite values.
Results may differ from a plain program's by a relative error of at most 0.0058.
Values may be sent and summed in bfloat16 or wider, within the bound.
No kernel may reach another device: no remote copies, remote signals or barrier semaphores. Data moves between devices by JAX's collectives and lax.ppermute only.
A program may use at most 128 MiB of HBM per device.

v0:
```python
import jax
import jax.numpy as jnp
from jax import lax
from jax.experimental import pallas as pl
from jax.experimental.pallas import tpu as pltpu
from jax.sharding import PartitionSpec as P


NORM_EPS = 1e-05
PAIR = 2
CHUNKS = 2
GROUP = 16
BATCH = 8

BLOCK = 4

F32 = jnp.float32
BF16 = jnp.bfloat16


def silu(value):
    return value / (1.0 + jnp.exp(-value))


def halves(value):
    high = value.astype(BF16)
    return high, (value - high.astype(F32)).astype(BF16)


def dot_nn(left, right):
    return lax.dot_general(left, right, (((1,), (0,)), ((), ())), preferred_element_type=F32)


def dot_nt(left, right):
    return lax.dot_general(left, right, (((1,), (1,)), ((), ())), preferred_element_type=F32)


def dot_tn(left, right):
    return lax.dot_general(left, right, (((0,), (0,)), ((), ())), preferred_element_type=F32)


def params(megabytes=62):
    return pltpu.CompilerParams(vmem_limit_bytes=megabytes * 1024 * 1024)


def cost(flops, moved, transcendentals=0):
    return pl.CostEstimate(
        flops=int(flops), bytes_accessed=int(moved), transcendentals=int(transcendentals)
    )


def convolve(ext_ref, kernel_rows, offset, tokens):
    summed = offset + kernel_rows[0:1] * ext_ref[5 : 5 + tokens]
    for tap in range(1, 4):
        summed = summed + kernel_rows[tap : tap + 1] * ext_ref[5 + tap : 5 + tap + tokens]
    return silu(summed)


def pack(slots, rank_here, map_slice, step_rows, rows_in, slot_total):
    sessions, tokens, channels = rows_in.shape
    _, group_tokens, map_width = map_slice.shape
    width = channels // CHUNKS
    extra = max(group_tokens, 8)

    def body(slot_ref, rank_ref, map_ref, step_ref, in_ref, *rest):
        outs = rest[:CHUNKS]
        small_sc, step_sc, sems, small_sem = rest[CHUNKS:]

        def copies(q):
            slot = slot_ref[q]
            return [
                pltpu.make_async_copy(
                    in_ref.at[q, :, k * width : (k + 1) * width],
                    outs[k].at[slot, 0:tokens, :],
                    sems.at[k * sessions + q],
                )
                for k in range(CHUNKS)
            ]

        for q in range(sessions):
            for copy in copies(q):
                copy.start()
        for q in range(sessions):
            home = slot_ref[q] // PAIR
            rank = slot_ref[q] % PAIR
            step_sc[home, pl.ds(rank, 1), :] = step_ref[q : q + 1, :]

            @pl.when(rank == rank_ref[0])
            def _():
                small_sc[home, 0, 0:group_tokens] = map_ref[q]

        small_sc[:, 1, 0:8] = step_sc[...].astype(BF16)
        smalls = [
            pltpu.make_async_copy(
                small_sc.at[home], outs[0].at[pl.ds(home * PAIR, PAIR), tokens:, :], small_sem.at[home]
            )
            for home in range(slot_total // PAIR)
        ]
        for copy in smalls:
            copy.start()
        for q in range(sessions):
            for copy in copies(q):
                copy.wait()
        for copy in smalls:
            copy.wait()

    vmem = pl.BlockSpec(memory_space=pltpu.VMEM)
    smem = pl.BlockSpec(memory_space=pltpu.SMEM)
    return pl.pallas_call(
        body,
        out_shape=[
            jax.ShapeDtypeStruct((slot_total, tokens + (extra if k == 0 else 0), width), BF16)
            for k in range(CHUNKS)
        ],
        in_specs=[smem, smem, vmem, vmem, vmem],
        out_specs=[pl.BlockSpec(memory_space=pl.ANY)] * CHUNKS,
        scratch_shapes=[
            pltpu.VMEM((slot_total // PAIR, PAIR, extra, map_width), BF16),
            pltpu.VMEM((slot_total // PAIR, 8, map_width), F32),
            pltpu.SemaphoreType.DMA((CHUNKS * sessions,)),
            pltpu.SemaphoreType.DMA((slot_total // PAIR,)),
        ],
        compiler_params=params(),
        cost_estimate=cost(0, 4 << 20),
        name="pack",
    )(slots, rank_here, map_slice, step_rows, rows_in)


def prepare(slots, lens, maps, fresh, map_window, state, map_kernel, map_bias, bias, decay):
    sessions, heads, head_dim, state_dim = state.shape
    groups, rows, group_tokens, width = maps.shape
    side = groups // PAIR
    tokens = side * group_tokens
    spread = heads * tokens
    channels = heads * head_dim
    chunk_heads = heads // CHUNKS
    chunk_spread = chunk_heads * tokens
    maps = maps.reshape(PAIR, side, rows, group_tokens, width)

    def per_head(values, size):
        lane = lax.broadcasted_iota(jnp.int32, (1, heads * size), 1) // size
        row = jnp.zeros((1, heads * size), F32)
        for h in range(heads):
            row = jnp.where(lane == h, values[h], row)
        return row

    def blocks(columns, size):
        row = lax.broadcasted_iota(jnp.int32, (spread, columns), 0) // tokens
        column = lax.broadcasted_iota(jnp.int32, (spread, columns), 1) // size
        return jnp.where(row == column, 1.0, 0.0).astype(BF16)

    def body(slot_ref, len_ref, *refs):
        map_refs = refs[:BATCH]
        (
            small_ref, win_ref, state_ref, kern_ref, off_ref, bias_ref, rate_ref,
            mat_ref, part_ref, wx_ref, in_ref, last_ref, tail_ref,
            raw_sc, valid_sc, step_sc, log_sc, weight_sc, same_ref, wide_ref,
        ) = refs[BATCH : BATCH + 20]
        exts = refs[BATCH + 20 :]
        lane = lax.broadcasted_iota(jnp.int32, (1, spread), 1) % tokens

        @pl.when(pl.program_id(0) == 0)
        def _():
            same_ref[...] = blocks(spread, tokens)
            wide_ref[...] = blocks(channels, head_dim)
            for s in range(sessions):
                slot = slot_ref[s]
                pair = small_ref[slot // PAIR * PAIR + 1].astype(F32)
                raw_sc[s : s + 1, :] = jnp.where(slot % PAIR == 0, pair[0:1], pair[1:2])
                valid_sc[s : s + 1, :] = jnp.where(lane < len_ref[s], 1.0, 0.0)
            step = jax.nn.softplus(raw_sc[...] + per_head(bias_ref, tokens)) * valid_sc[...]
            fall = -per_head(rate_ref, tokens) * step
            log = fall
            rest = jnp.where(lane < tokens - 1, pltpu.roll(fall, spread - 1, 1), 0.0)
            hop = 1
            while hop < tokens:
                log = log + jnp.where(lane >= hop, pltpu.roll(log, hop, 1), 0.0)
                rest = rest + jnp.where(lane < tokens - hop, pltpu.roll(rest, spread - hop, 1), 0.0)
                hop *= 2
            step_sc[...] = step
            log_sc[...] = log
            weight_sc[...] = jnp.exp(rest) * step

        token = lax.broadcasted_iota(jnp.int32, (tokens, spread), 0)
        within = lax.broadcasted_iota(jnp.int32, (tokens, spread), 1) % tokens
        diagonal = within == token
        causal = within <= token
        final = lax.broadcasted_iota(jnp.int32, (heads, spread), 1) == (
            lax.broadcasted_iota(jnp.int32, (heads, spread), 0) * tokens + tokens - 1
        )
        for i in range(BATCH):
            c = pl.program_id(0) * BATCH + i
            ext_sc = exts[i]
            step = step_sc[pl.ds(c, 1), :]
            log = log_sc[pl.ds(c, 1), :]
            weight = weight_sc[pl.ds(c, 1), :]
            ext_sc[5:8] = win_ref[i].astype(F32)
            ext_sc[8:] = map_refs[i][0, :, 0].astype(F32).reshape(tokens, width)
            tail_ref[i] = jnp.concatenate(
                [ext_sc[pl.ds(len_ref[c] + 5 + n, 1), :] for n in range(3)], axis=0
            ).astype(BF16)
            conv = convolve(ext_sc, kern_ref[...], off_ref[...], tokens)
            in_high, in_low = halves(conv[:, :state_dim])
            out_high, out_low = halves(conv[:, state_dim:])
            in_ref[i] = jnp.concatenate([in_high, in_low, in_high], axis=0)

            log_all = jnp.broadcast_to(log, (tokens, spread))
            spot = jnp.where(diagonal, log_all, 0.0)
            first = spot.astype(BF16)
            second, third = halves(spot - first.astype(F32))
            own = dot_nn(jnp.concatenate([first, second, third], axis=0), same_ref[...])
            own = own[:tokens] + own[tokens : 2 * tokens] + own[2 * tokens :]
            decay = jnp.where(causal, jnp.exp(jnp.where(causal, own - log_all, 0.0)), 0.0)
            keys = jnp.concatenate([jnp.concatenate([in_high, in_low], axis=1)] * heads, axis=0)
            asks = jnp.concatenate(
                [
                    jnp.concatenate([out_high, out_high], axis=1),
                    jnp.concatenate([out_low, jnp.zeros_like(out_low)], axis=1),
                ],
                axis=0,
            )
            scores = dot_nt(asks, keys)
            scores = scores[:tokens] + scores[tokens:]
            high, low = halves(decay * scores * step)
            for k in range(CHUNKS):
                part = slice(k * chunk_spread, (k + 1) * chunk_spread)
                base = 2 * k * chunk_spread
                mat_ref[i, :, base : base + chunk_spread] = high[:, part]
                mat_ref[i, :, base + chunk_spread : base + 2 * chunk_spread] = low[:, part]

            rise = halves(jnp.where(diagonal, jnp.exp(log_all), 0.0))
            load = halves(jnp.where(diagonal, jnp.broadcast_to(weight, (tokens, spread)), 0.0))
            grown = dot_nn(jnp.concatenate([*rise, *load], axis=0), wide_ref[...])
            wx_ref[i] = grown[2 * tokens : 3 * tokens] + grown[3 * tokens :]
            carried = dot_nt(
                jnp.concatenate([out_high, out_low], axis=0), state_ref[i].reshape(channels, state_dim)
            )
            part_ref[i] = (carried[:tokens] + carried[tokens:]) * (
                grown[:tokens] + grown[tokens : 2 * tokens]
            )
            last = jnp.sum(jnp.where(final, jnp.exp(log), 0.0), axis=1, keepdims=True)
            last_ref[i] = jnp.broadcast_to(last, (heads, 128))

    def whole(*shape):
        return pl.BlockSpec(shape, lambda g, s, n: (0,) * len(shape))

    def at(*shape):
        return pl.BlockSpec((BATCH,) + shape, lambda g, s, n: (g,) + (0,) * len(shape))

    def received(i):
        return pl.BlockSpec(
            (1, side, 1, group_tokens, width),
            lambda g, s, n: (s[g * BATCH + i] % PAIR, 0, s[g * BATCH + i] // PAIR, 0, 0),
        )

    return pl.pallas_call(
        body,
        out_shape=[
            jax.ShapeDtypeStruct((sessions, tokens, 2 * spread), BF16),
            jax.ShapeDtypeStruct((sessions, tokens, channels), F32),
            jax.ShapeDtypeStruct((sessions, tokens, channels), F32),
            jax.ShapeDtypeStruct((sessions, 3 * tokens, state_dim), BF16),
            jax.ShapeDtypeStruct((sessions, heads, 128), F32),
            jax.ShapeDtypeStruct((sessions, 3, width), BF16),
        ],
        grid_spec=pltpu.PrefetchScalarGridSpec(
            num_scalar_prefetch=2,
            grid=(sessions // BATCH,),
            in_specs=[received(i) for i in range(BATCH)]
            + [
                pl.BlockSpec((rows * PAIR, 8, width), lambda g, s, n: (0, tokens // 8, 0)),
                at(3, width),
                at(heads, head_dim, state_dim),
                whole(4, width),
                whole(1, width),
                pl.BlockSpec(memory_space=pltpu.SMEM),
                pl.BlockSpec(memory_space=pltpu.SMEM),
            ],
            out_specs=[
                at(tokens, 2 * spread),
                at(tokens, channels),
                at(tokens, channels),
                at(3 * tokens, state_dim),
                at(heads, 128),
                at(3, width),
            ],
            scratch_shapes=[pltpu.VMEM((sessions, spread), F32)] * 5
            + [pltpu.VMEM((spread, spread), BF16), pltpu.VMEM((spread, channels), BF16)]
            + [pltpu.VMEM((tokens + 8, width), F32)] * BATCH,
        ),
        compiler_params=params(),
        cost_estimate=cost(sessions * (1 << 25), sessions << 19),
        name="prepare",
    )(
        slots, lens, *[maps] * BATCH, fresh, map_window, state, map_kernel, map_bias, bias, decay
    )


def mix(k, slots, lens, fresh, window, prepared, state, kernel, offset, skip, earlier):
    mats, parts, loads, in_maps, lasts = prepared
    slot_total, _, width = fresh.shape
    tokens = mats.shape[1]
    sessions, heads, head_dim, state_dim = state.shape
    chunk_heads = heads // CHUNKS
    chunk_spread = chunk_heads * tokens
    channels = heads * head_dim

    def body(slot_ref, len_ref, *refs):
        new_refs = refs[:BATCH]
        (
            win_ref, mat_ref, part_ref, wx_ref, in_ref, last_ref, state_ref, kern_ref, off_ref, skip_ref,
        ) = refs[BATCH : BATCH + 10]
        y_ref, next_ref, tail_ref, y_sc, sems, *exts = refs[BATCH + 10 + len(earlier) :]
        g = pl.program_id(0)
        turn = g % 2

        def copy(i, group, half):
            return pltpu.make_async_copy(
                y_sc.at[half, i], y_ref.at[slot_ref[group * BATCH + i]], sems.at[half, i]
            )

        @pl.when(g >= 2)
        def _():
            for i in range(BATCH):
                copy(i, g - 2, turn).wait()

        owner = lax.broadcasted_iota(jnp.int32, (chunk_spread, width), 0) // tokens
        lane = lax.broadcasted_iota(jnp.int32, (chunk_spread, width), 1) // head_dim
        own = owner == lane
        zero = jnp.zeros((chunk_spread, width), BF16)
        token = lax.broadcasted_iota(jnp.int32, (tokens, width), 0)
        skip_lane = lax.broadcasted_iota(jnp.int32, (1, width), 1) // head_dim
        skip_row = jnp.zeros((1, width), F32)
        for h in range(chunk_heads):
            skip_row = jnp.where(skip_lane == h, skip_ref[k * chunk_heads + h], skip_row)
        for i in range(BATCH):
            c = g * BATCH + i
            ext_sc = exts[i]
            ext_sc[5:8] = win_ref[i].astype(F32)
            ext_sc[8:] = new_refs[i][0].astype(F32)
            tail_ref[i] = jnp.concatenate(
                [ext_sc[pl.ds(len_ref[c] + 5 + n, 1), :] for n in range(3)], axis=0
            ).astype(BF16)
            x = convolve(ext_sc, kern_ref[...], off_ref[...], tokens)
            high, low = halves(x)
            tall_high = jnp.where(own, jnp.concatenate([high] * chunk_heads, axis=0), zero)
            tall_low = jnp.where(own, jnp.concatenate([low] * chunk_heads, axis=0), zero)
            mat = mat_ref[i]
            inside = dot_nn(
                jnp.concatenate([mat, mat[:, :chunk_spread]], axis=1),
                jnp.concatenate([tall_high, tall_high, tall_low], axis=0),
            )
            mixed = inside + part_ref[i] + skip_row * x
            y_sc[turn, i] = jnp.where(token < len_ref[c], mixed, 0.0).astype(BF16)
            copy(i, g, turn).start()
            w_high, w_low = halves(x * wx_ref[i])
            added = dot_tn(jnp.concatenate([w_high, w_high, w_low], axis=0), in_ref[i])
            for h in range(chunk_heads):
                at = k * chunk_heads + h
                next_ref[i, h] = (
                    last_ref[i, at : at + 1, :] * state_ref[i, h].astype(F32)
                    + added[h * head_dim : (h + 1) * head_dim]
                ).astype(BF16)

        @pl.when(g == pl.num_programs(0) - 1)
        def _():
            for i in range(BATCH):
                copy(i, g - 1, 1 - turn).wait()
                copy(i, g, turn).wait()

    def whole(*shape):
        return pl.BlockSpec(shape, lambda g, s, n: (0,) * (len(shape) - 1) + (k,))

    def cut(*shape):
        return pl.BlockSpec((BATCH,) + shape, lambda g, s, n: (g,) + (0,) * (len(shape) - 1) + (k,))

    def at(*shape):
        return pl.BlockSpec((BATCH,) + shape, lambda g, s, n: (g,) + (0,) * len(shape))

    def received(i):
        return pl.BlockSpec((1, tokens, width), lambda g, s, n: (s[g * BATCH + i], 0, 0))

    held = pl.BlockSpec((BATCH, chunk_heads, head_dim, state_dim), lambda g, s, n: (g, k, 0, 0))
    anywhere = pl.BlockSpec(memory_space=pl.ANY)
    operands = [slots, lens, *[fresh] * BATCH, window, mats, parts, loads, in_maps, lasts]
    operands += [state, kernel, offset, skip]
    return pl.pallas_call(
        body,
        out_shape=[
            jax.ShapeDtypeStruct((slot_total, tokens, width), BF16),
            jax.ShapeDtypeStruct(state.shape, BF16),
            jax.ShapeDtypeStruct((sessions, 3, channels), BF16),
        ],
        grid_spec=pltpu.PrefetchScalarGridSpec(
            num_scalar_prefetch=2,
            grid=(sessions // BATCH,),
            in_specs=[received(i) for i in range(BATCH)]
            + [
                cut(3, width),
                cut(tokens, 2 * chunk_spread),
                cut(tokens, width),
                cut(tokens, width),
                at(3 * tokens, state_dim),
                at(heads, 128),
                held,
                whole(4, width),
                whole(1, width),
                pl.BlockSpec(memory_space=pltpu.SMEM),
            ]
            + [anywhere] * len(earlier),
            out_specs=[anywhere, held, cut(3, width)],
            scratch_shapes=[
                pltpu.VMEM((2, BATCH, tokens, width), BF16),
                pltpu.SemaphoreType.DMA((2, BATCH)),
            ]
            + [pltpu.VMEM((tokens + 8, width), F32)] * BATCH,
        ),
        input_output_aliases={len(operands) + i: 1 + i for i in range(len(earlier))},
        compiler_params=params(),
        cost_estimate=cost(sessions * (1 << 24), sessions << 19),
    )(*operands, *earlier)


def block_height(tokens):
    return BLOCK // 2 * tokens + 8


def gate_rows(k, slots, picks, back, gate, adapters, scale, earlier):
    sessions, tokens, _ = gate.shape
    _, _, width = back.shape
    rank = adapters.shape[1] // 2
    height = block_height(tokens)

    def body(slot_ref, pick_ref, *refs):
        backs, downs = refs[:GROUP], refs[GROUP : 2 * GROUP]
        gate_ref, scale_ref = refs[2 * GROUP : 2 * GROUP + 2]
        sum_ref, gated_ref = refs[-2:]
        ones = jnp.ones((8, width), BF16)
        lows, squares = [], []
        for i in range(GROUP):
            gated = backs[i][0].astype(F32) * silu(gate_ref[i].astype(F32))
            gated_ref[i] = gated
            low = dot_nt((gated * scale_ref[...]).astype(BF16), downs[i][0])
            high, rest = halves(gated * gated)
            lows.append(low)
            squares.append(dot_nt(ones, high) + dot_nt(ones, rest))
        for b in range(GROUP // BLOCK):
            rows = [
                jnp.concatenate(lows[i : i + 2], axis=1) for i in range(b * BLOCK, (b + 1) * BLOCK, 2)
            ]
            rows.append(jnp.concatenate(squares[b * BLOCK : (b + 1) * BLOCK], axis=1))
            both = jnp.concatenate(rows, axis=0)
            if earlier:
                both = both + refs[2 * GROUP + 2][b * height : (b + 1) * height]
            sum_ref[b * height : (b + 1) * height] = both

    def returned(i):
        return pl.BlockSpec((1, tokens, width), lambda g, s, a: (s[g * GROUP + i], 0, 0))

    def chosen(i):
        return pl.BlockSpec((1, rank, width), lambda g, s, a: (a[g * GROUP + i], 0, k))

    sums = pl.BlockSpec((GROUP // BLOCK * height, 128), lambda g, s, a: (g, 0))
    return pl.pallas_call(
        body,
        out_shape=[
            jax.ShapeDtypeStruct((sessions // BLOCK * height, 128), F32),
            jax.ShapeDtypeStruct((sessions, tokens, width), F32),
        ],
        grid_spec=pltpu.PrefetchScalarGridSpec(
            num_scalar_prefetch=2,
            grid=(sessions // GROUP,),
            in_specs=[returned(i) for i in range(GROUP)]
            + [chosen(i) for i in range(GROUP)]
            + [
                pl.BlockSpec((GROUP, tokens, width), lambda g, s, a: (g, 0, k)),
                pl.BlockSpec((1, width), lambda g, s, a: (0, k)),
            ]
            + [sums] * len(earlier),
            out_specs=[sums, pl.BlockSpec((GROUP, tokens, width), lambda g, s, a: (g, 0, 0))],
        ),
        compiler_params=params(),
        cost_estimate=cost(sessions * (1 << 22), sessions << 18),
    )(slots, picks, *[back] * GROUP, *[adapters] * GROUP, gate, scale, *earlier)


def finish(picks, gated, totals, adapters, scale, inner):
    sessions, tokens, width = gated[0].shape
    channels = width * CHUNKS
    rank = adapters.shape[1] // 2
    height = block_height(tokens)

    def body(pick_ref, *refs):
        ups, rows = refs[:GROUP], refs[GROUP : GROUP + CHUNKS]
        total_ref, scale_ref, out_ref, delta_ref = refs[GROUP + CHUNKS :]
        spot = lax.broadcasted_iota(jnp.int32, (tokens, tokens), 0) == lax.broadcasted_iota(
            jnp.int32, (tokens, tokens), 1
        )
        for i in range(GROUP):
            start = i // BLOCK * height
            j = i % BLOCK
            line = total_ref[start + height - 8 : start + height - 7, j * tokens : (j + 1) * tokens]
            square = jnp.sum(jnp.where(spot, line, 0.0), axis=1, keepdims=True)
            inverse = lax.rsqrt(square / inner + NORM_EPS)
            first = start + j // 2 * tokens
            low = total_ref[first : first + tokens, j % 2 * rank : (j % 2 + 1) * rank] * inverse
            for k in range(CHUNKS):
                part = slice(k * width, (k + 1) * width)
                out_ref[i, :, part] = (rows[k][i] * inverse * scale_ref[:, part]).astype(BF16)
            delta_ref[i] = dot_nn(low.astype(BF16), ups[i][0]).astype(BF16)

    def chosen(i):
        return pl.BlockSpec((1, rank, channels), lambda g, a: (a[g * GROUP + i], 1, 0))

    out = pl.BlockSpec((GROUP, tokens, channels), lambda g, a: (g, 0, 0))
    return pl.pallas_call(
        body,
        out_shape=[jax.ShapeDtypeStruct((sessions, tokens, channels), BF16)] * 2,
        grid_spec=pltpu.PrefetchScalarGridSpec(
            num_scalar_prefetch=1,
            grid=(sessions // GROUP,),
            in_specs=[chosen(i) for i in range(GROUP)]
            + [pl.BlockSpec((GROUP, tokens, width), lambda g, a: (g, 0, 0))] * CHUNKS
            + [
                pl.BlockSpec((GROUP // BLOCK * height, 128), lambda g, a: (g, 0)),
                pl.BlockSpec((1, channels), lambda g, a: (0, 0)),
            ],
            out_specs=[out, out],
        ),
        compiler_params=params(),
        cost_estimate=cost(sessions * (1 << 22), sessions << 18),
        name="finish",
    )(picks, *[adapters] * GROUP, *gated, totals, scale)


def exchange(value, axis, groups=None):
    return lax.all_to_all(
        value, axis, split_axis=0, concat_axis=0, tiled=True, axis_index_groups=groups
    )


def share_all(value, axis, count, groups=None):
    return exchange(
        jnp.broadcast_to(value[None], (count,) + value.shape).reshape((-1,) + value.shape[1:]), axis, groups
    )


def place(base, length, blocks):
    count = len(blocks)
    shape = blocks[0][0].shape

    def body(base_ref, *refs):
        ins, out_ref = refs[:count], refs[count]
        helds, sems = refs[count + 1 : 2 * count + 1], refs[2 * count + 1]
        loads = [pltpu.make_async_copy(ins[i], helds[i], sems.at[0, i]) for i in range(count)]
        for load in loads:
            load.start()
        stores = []
        for i, (_, behind, part) in enumerate(blocks):
            loads[i].wait()
            target = out_ref.at[(base_ref[0] + (length - behind)) % length]
            if part is not None:
                rest = (slice(None),) * (len(shape) - 2)
                target = target.at[(*rest, slice(part[0], part[1]))]
            stores.append(pltpu.make_async_copy(helds[i], target, sems.at[1, i]))
            stores[i].start()
        for store in stores:
            store.wait()

    return pl.pallas_call(
        body,
        out_shape=jax.ShapeDtypeStruct((length,) + shape, blocks[0][0].dtype),
        in_specs=[pl.BlockSpec(memory_space=pltpu.SMEM)]
        + [pl.BlockSpec(memory_space=pl.ANY)] * count,
        out_specs=pl.BlockSpec(memory_space=pl.ANY),
        scratch_shapes=[pltpu.VMEM(value.shape, value.dtype) for value, _, _ in blocks]
        + [pltpu.SemaphoreType.DMA((2, count))],
        compiler_params=params(),
        cost_estimate=cost(0, 4 * length * blocks[0][0].size),
    )(base.reshape(1), *[value for value, _, _ in blocks])


def shift(value, axis, rings, d):
    pairs = [(ring[i], ring[(i + d) % len(ring)]) for ring in rings for i in range(len(ring))]
    return lax.ppermute(value, axis, pairs)


def everyone(value, axis, rings):
    length = len(rings[0])
    return [(value, 0, None)] + [(shift(value, axis, rings, d), d, None) for d in range(1, length)]


def gather_adapters(block, row, size_z, size_x):
    along_z = [[z * size_x + x for z in range(size_z)] for x in range(size_x)]
    along_x = [[z * size_x + x for x in range(size_x)] for z in range(size_z)]
    size = block.shape[0]
    half = size // 2
    column = place(row // size_x, size_z, everyone(block, "row", along_z))
    parts = [(column, 0, None), (shift(column, "row", along_x, 1), 1, None)]
    if size_x == 4:
        behind = parts[1][0]
        ahead = shift(column, "row", along_x, 3)
        parts.append((ahead, 3, None))
        parts.append((shift(behind[:, :half], "row", along_x, 1), 2, (0, half)))
        parts.append((shift(ahead[:, half:], "row", along_x, 3), 2, (half, size)))
    whole = place(row % size_x, size_x, parts)
    return whole.reshape((size_z * size_x,) + block.shape)


def shards(
    channel_rows_in,
    gate_rows_in,
    map_input_rows,
    step_size_input,
    channel_kernel_weight,
    map_kernel_weight,
    channel_conv_bias,
    map_kernel_bias,
    step_size_bias,
    head_decay_rate,
    head_skip_weight,
    gated_norm_scale,
    scan_state_cache,
    channel_window_cache,
    map_window_cache,
    adapter_down_weight,
    adapter_up_weight,
    session_slot_index,
    lengths,
    session_adapter_index,
):
    sessions, tokens, channels = channel_rows_in.shape
    heads = step_size_input.shape[1]
    rows = lax.axis_size("row")
    sections = lax.axis_size("section")
    row = lax.axis_index("row")
    section = lax.axis_index("section")
    size_x = 4 if rows >= 32 else 2
    size_z = rows // size_x
    side = sections // PAIR
    group_tokens = tokens // side

    local = jnp.arange(sessions, dtype=jnp.int32)
    mine = lax.dynamic_slice_in_dim(session_slot_index, row * sessions, sessions)
    homes = mine // sessions
    sooner = (homes[None, :] == homes[:, None]) & (local[None, :] < local[:, None])
    serve_slots = homes * PAIR + jnp.sum(sooner.astype(jnp.int32), axis=1)
    here = (session_slot_index // sessions == row).astype(jnp.int32).reshape(rows, sessions)
    ahead = jnp.sum(
        jnp.where(local[None, None, :] < local[None, :, None], here[:, None, :], 0), axis=2
    )
    target = (jnp.arange(rows, dtype=jnp.int32)[:, None] * PAIR + ahead).reshape(-1)
    match = session_slot_index[None, :] == (row * sessions + local)[:, None]
    home_slots = jnp.sum(jnp.where(match, target[None, :], 0), axis=1)
    home_lens = jnp.sum(jnp.where(match, lengths[None, :], 0), axis=1)
    adapter = lax.dynamic_slice_in_dim(session_adapter_index, row * sessions, sessions)
    picks = adapter % size_x * size_z + adapter // size_x

    map_slice = lax.dynamic_slice_in_dim(
        map_input_rows, section % side * group_tokens, group_tokens, axis=1
    )
    step_rows = step_size_input.reshape(sessions, heads * tokens).astype(F32)
    sent = pack(
        serve_slots, (section // side).reshape(1), map_slice, step_rows, channel_rows_in, rows * PAIR
    )
    fresh = []
    for k in range(CHUNKS):
        fresh.append(exchange(sent[k], "row"))
    block = jnp.concatenate([adapter_down_weight[0], adapter_up_weight[0]], axis=0)
    block, home_slots, home_lens, picks = lax.optimization_barrier((block, home_slots, home_lens, picks))
    adapters = gather_adapters(block, row, size_z, size_x)
    share = fresh[0].reshape((rows, PAIR) + fresh[0].shape[1:])[:, 0, tokens : tokens + group_tokens]
    maps = place(section, sections, everyone(share, "section", [list(range(sections))]))
    *prepared, map_window_next = prepare(
        home_slots,
        home_lens,
        maps,
        fresh[0],
        map_window_cache,
        scan_state_cache,
        map_kernel_weight,
        map_kernel_bias[None],
        step_size_bias,
        head_decay_rate,
    )
    scale = gated_norm_scale[None]
    back = []
    carried = []
    for k in range(CHUNKS):
        mixed, *carried = mix(
            k,
            home_slots,
            home_lens,
            fresh[k],
            channel_window_cache,
            prepared,
            scan_state_cache,
            channel_kernel_weight,
            channel_conv_bias[None],
            head_skip_weight,
            carried,
        )
        back.append(exchange(mixed, "row"))
    scan_state_next, channel_window_next = carried
    sums = []
    gated = []
    for k in range(CHUNKS):
        total, part = gate_rows(k, serve_slots, picks, back[k], gate_rows_in, adapters, scale, sums)
        sums = [total]
        gated.append(part)
    total = exchange(sums[0], "section")
    total = jnp.sum(total.reshape(sections, -1, 128), axis=0)
    totals = share_all(total, "section", sections)
    mixer_output_rows, adapter_delta = finish(
        picks, gated, totals, adapters, scale, channels * sections
    )
    return (mixer_output_rows, adapter_delta, scan_state_next, channel_window_next, map_window_next)


def solution(mesh):
    split = P("row", None, "section")
    return jax.shard_map(
        shards,
        mesh=mesh,
        in_specs=(
            split,
            split,
            P("row", None, None),
            P("row", "section", None),
            P(None, "section"),
            P(),
            P("section"),
            P(),
            P("section"),
            P("section"),
            P("section"),
            P("section"),
            P("row", "section", None, None),
            split,
            P("row", None, None),
            split,
            split,
            P(),
            P(),
            P(),
        ),
        out_specs=(
            split,
            split,
            P("row", "section", None, None),
            split,
            P("row", None, None),
        ),
        check_vma=False,
    )
```

profile of v0, /device:TPU:2, one launch (start us, length us, event | category | flops | bytes accessed | tf_op | source)
XLA Modules:
  0.0 279.6 jit_solution(15115689094999001353)
XLA Ops:
  5.2 3.5 %pack.1 = (bf16[64,40,256]{2,1,0:T(8,128)(2,1)}, bf16[64,32,256]{2,1,0:T(8,128)(2,1)}) custom-call(s32[32]{0:T(128)} %multiply_add_fusion.slot_ref, s32[1]{0:T(128)} %bitcast.5.rank_ref, bf16[32,8,256]{2,1,0:T(8,128)(2,1)} %constant_dynamic-slice_fusion.map_ref, f32[32,256]{1,0:T(8,128)} %reshape.92.step_ref, bf16[32,32,512]{2,1,0:T(8,128)(2,1)} %in_ref.1), custom_call_target="tpu_custom_call" | custom-call | bytes 4194304 | tf_op jit(solution)/shard_map/pack/pallas_call | solution.py:109
  8.8 45.4 %all_to_all.37.refs_8_.refs_0_.refs_1_.refs_2_.refs_3_.refs_4_.refs_5_.refs_6_.refs_7_ = bf16[64,40,256]{2,1,0:T(8,128)(2,1)S(1)} all-to-all(bf16[64,40,256]{2,1,0:T(8,128)(2,1)} %get-tuple-element.33), channel_id=1, replica_groups=mesh['section'=8,'row'=32] {'row'}, dimensions={0} | all-to-all | bytes 2621440 | tf_op jit(solution)/shard_map/all_to_all | solution.py:537
  54.2 6.2 %all-to-all-start.2 = ((bf16[64,32,256]{2,1,0:T(8,128)(2,1)}), bf16[64,32,256]{2,1,0:T(8,128)(2,1)}, u32[]{:S(2)}, u32[]{:S(2)}) async-start(bf16[64,32,256]{2,1,0:T(8,128)(2,1)} %get-tuple-element.41), calls=%async_computation.2 | async-start | bytes 2097152 | tf_op jit(solution)/shard_map/all_to_all | solution.py:537
  80.7 10.0 %prepare.1 = (bf16[32,32,512]{2,1,0:T(8,128)(2,1)}, f32[32,32,512]{2,1,0:T(8,128)}, f32[32,32,512]{2,1,0:T(8,128)}, bf16[32,96,128]{2,1,0:T(8,128)(2,1)}, f32[32...) custom-call(s32[32]{0:T(128)} %get-tuple-element.31.slot_ref, s32[32]{0:T(128)} %get-tuple-element.32.len_ref, ...), custom_call_target="tpu_custom_call" | custom-call | flops 1073741824 | bytes 16777216 | tf_op jit(solution)/shard_map/prepare/pallas_call | solution.py:256
  90.7 8.3 %shard_map.230 = (bf16[64,32,256]{2,1,0:T(8,128)(2,1)}, bf16[32,8,64,128]{3,2,1,0:T(8,128)(2,1)}, bf16[32,3,512]{2,1,0:T(4,128)(2,1)}) custom-call(s32[32]{0:T(128)} %get-tuple-element.31.slot_ref, s32[32]{0:T(128)} %get-tuple-element.32.len_ref, bf16[64,40,256]{2,1,0:T(8,128)(2,1)} %copy-done.2, bf16[64,40,256]{2,1,0:T(8,128)(2,1)} %copy-done.2, ...), custom_call_target="tpu_custom_call" | custom-call | flops 536870912 | bytes 16777216 | tf_op jit(solution)/shard_map/pallas_call | solution.py:387
  99.0 9.9 %all-to-all-start.1 = ((bf16[64,32,256]{2,1,0:T(8,128)(2,1)}), bf16[64,32,256]{2,1,0:T(8,128)(2,1)S(1)}, u32[]{:S(2)}, u32[]{:S(2)}) async-start(bf16[64,32,256]{2,1,0:T(8,128)(2,1)} %get-tuple-element.39), calls=%async_computation.1 | async-start | bytes 2097152 | tf_op jit(solution)/shard_map/all_to_all | solution.py:537
  108.9 8.3 %shard_map.232 = (bf16[64,32,256]{2,1,0:T(8,128)(2,1)}, bf16[32,8,64,128]{3,2,1,0:T(8,128)(2,1)}, bf16[32,3,512]{2,1,0:T(4,128)(2,1)}) custom-call(s32[32]{0:T(128)} %get-tuple-element.31.slot_ref, s32[32]{0:T(128)} %get-tuple-element.32.len_ref, ...), custom_call_target="tpu_custom_call", output_to_operand_aliasing={{1}: (20, {}), {2}: (21, {})} | custom-call | flops 536870912 | bytes 16777216 | tf_op jit(solution)/shard_map/pallas_call | solution.py:387
  117.1 20.3 %all-to-all-done.1.refs_0_.refs_1_.refs_2_.refs_3_.refs_4_.refs_5_.refs_6_.refs_7_.refs_8_.refs_9_.refs_10_.refs_11_.refs_12_.refs_13_.refs_14_.refs_15_ = bf16[64,32,256]{2,1,0:T(8,128)(2,1)S(1)} async-done(((bf16[64,32,256]{2,1,0:T(8,128)(2,1)}), bf16[64,32,256]{2,1,0:T(8,128)(2,1)S(1)}, u32[]{:S(2)}, u32[]{:S(2)}) %all-to-all-start.1) | async-done | bytes 1048608 | tf_op jit(solution)/shard_map/all_to_all | solution.py:537
  137.4 6.3 %all-to-all-start.3 = ((bf16[64,32,256]{2,1,0:T(8,128)(2,1)}), bf16[64,32,256]{2,1,0:T(8,128)(2,1)}, u32[]{:S(2)}, u32[]{:S(2)}) async-start(bf16[64,32,256]{2,1,0:T(8,128)(2,1)} %get-tuple-element.44), calls=%async_computation.3 | async-start | bytes 2097152 | tf_op jit(solution)/shard_map/all_to_all | solution.py:537
  147.8 2.7 collective-permute-start.2
  152.9 2.7 collective-permute-start.4
  155.6 18.1 %collective-permute-done.refs_1_ = bf16[128,512]{1,0:T(8,128)(2,1)S(1)} collective-permute-done((bf16[128,512]{1,0:T(8,128)(2,1)S(1)}, bf16[128,512]{1,0:T(8,128)(2,1)S(1)}, u32[]{:S(2)}, u32[]{:S(2)}) %collective-permute-start) | collective-permute-done | bytes 131104 | tf_op jit(solution)/shard_map/ppermute | solution.py:585
  175.3 5.3 %collective-permute-done.1.refs_2_ = bf16[128,512]{1,0:T(8,128)(2,1)S(1)} collective-permute-done((bf16[128,512]{1,0:T(8,128)(2,1)S(1)}, bf16[128,512]{1,0:T(8,128)(2,1)S(1)}, u32[]{:S(2)}, u32[]{:S(2)}) %collective-permute-start.1) | collective-permute-done | bytes 131104 | tf_op jit(solution)/shard_map/ppermute | solution.py:585
  181.1 6.3 %collective-permute-done.2.refs_3_ = bf16[128,512]{1,0:T(8,128)(2,1)S(1)} collective-permute-done((bf16[128,512]{1,0:T(8,128)(2,1)S(1)}, bf16[128,512]{1,0:T(8,128)(2,1)S(1)}, u32[]{:S(2)}, u32[]{:S(2)}) %collective-permute-start.2) | collective-permute-done | bytes 131104 | tf_op jit(solution)/shard_map/ppermute | solution.py:585
  187.3 4.6 %collective-permute-done.3.refs_4_ = bf16[128,512]{1,0:T(8,128)(2,1)S(1)} collective-permute-done((bf16[128,512]{1,0:T(8,128)(2,1)S(1)}, bf16[128,512]{1,0:T(8,128)(2,1)S(1)}, u32[]{:S(2)}, u32[]{:S(2)}) %collective-permute-start.3) | collective-permute-done | bytes 131104 | tf_op jit(solution)/shard_map/ppermute | solution.py:585
  197.5 22.6 %collective-permute-done.8.refs_2_ = bf16[8,128,512]{2,1,0:T(8,128)(2,1)S(1)} collective-permute-done((bf16[8,128,512]{2,1,0:T(8,128)(2,1)}, bf16[8,128,512]{2,1,0:T(8,128)(2,1)S(1)}, u32[]{:S(2)}, u32[]{:S(2)}) %collective-permute-start.8) | collective-permute-done | bytes 1048608 | tf_op jit(solution)/shard_map/ppermute | solution.py:585
  223.4 10.3 %collective-permute-done.10.refs_4_ = bf16[8,64,512]{2,1,0:T(8,128)(2,1)} collective-permute-done((bf16[8,64,512]{2,1,0:T(8,128)(2,1)S(1)}, bf16[8,64,512]{2,1,0:T(8,128)(2,1)}, u32[]{:S(2)}, u32[]{:S(2)}) %collective-permute-start.10) | collective-permute-done | bytes 524320 | tf_op jit(solution)/shard_map/ppermute | solution.py:585
  235.9 3.3 %shard_map.228 = bf16[4,8,128,512]{3,2,1,0:T(8,128)(2,1)} custom-call(s32[1]{0:T(128)} %bitcast.2.base_ref, bf16[8,128,512]{2,1,0:T(8,128)(2,1)} %shard_map.227.refs_0_, bf16[8,128,512]{2,1,0:T(8,128)(2,1)} %copy-done.4, bf16[8,128,512]{2,1,0:T(8,128)(2,1)} %copy-done.3, bf16[8,64,512]{2,1,0:T(8,128)(2,1)} %collective-permute-done.9.refs_3_, ...), custom_call_target="tpu_custom_call" | custom-call | bytes 8388608 | tf_op jit(solution)/shard_map/pallas_call | solution.py:570
  239.3 4.5 %shard_map.231 = (f32[576,128]{1,0:T(8,128)}, f32[32,32,256]{2,1,0:T(8,128)}) custom-call(s32[32]{0:T(128)} %multiply_add_fusion.slot_ref, s32[32]{0:T(128)} %fusion.7.pick_ref, bf16[64,32,256]{2,1,0:T(8,128)(2,1)} %copy-done.1, bf16[64,32,256]{2,1,0:T(8,128)(2,1)} %copy-done.1, bf16[64,32,256]{2,1,0:T(8,128)(2,1)} %copy-done.1, ...), custom_call_target="tpu_custom_call" | custom-call | flops 134217728 | bytes 8388608 | tf_op jit(solution)/shard_map/pallas_call | solution.py:464
  243.8 4.6 %shard_map.233 = (f32[576,128]{1,0:T(8,128)}, f32[32,32,256]{2,1,0:T(8,128)}) custom-call(s32[32]{0:T(128)} %multiply_add_fusion.slot_ref, s32[32]{0:T(128)} %fusion.7.pick_ref, bf16[64,32,256]{2,1,0:T(8,128)(2,1)} %all-to-all-done.3.refs_0_.refs_1_.refs_2_.refs_3_.refs_4_.refs_5_.refs_6_.refs_7_.refs_8_.refs_9_.refs_10_.refs_11_.refs_12_.refs_13_.refs_14_.refs_15_, ...), custom_call_target="tpu_custom_call" | custom-call | flops 134217728 | bytes 8388608 | tf_op jit(solution)/shard_map/pallas_call | solution.py:464
  248.4 13.4 %all_to_all.38 = f32[8,72,128]{2,1,0:T(8,128)S(1)} all-to-all(f32[8,72,128]{2,1,0:T(8,128)} %bitcast.76), channel_id=1, replica_groups=mesh['section'=8,'row'=32] {'section'}, dimensions={0} | all-to-all | bytes 589824 | tf_op jit(solution)/shard_map/all_to_all | solution.py:537
  262.6 3.4 %all-to-all-start.5 = ((f32[8,72,128]{2,1,0:T(8,128)}), f32[8,72,128]{2,1,0:T(8,128)S(1)}, u32[]{:S(2)}, u32[]{:S(2)}) async-start(f32[8,72,128]{2,1,0:T(8,128)} %broadcast_in_dim.80), calls=%async_computation.5 | async-start | bytes 589824 | tf_op jit(solution)/shard_map/all_to_all | solution.py:537
  267.4 6.5 %all-to-all-done.5 = f32[8,72,128]{2,1,0:T(8,128)S(1)} async-done(((f32[8,72,128]{2,1,0:T(8,128)}), f32[8,72,128]{2,1,0:T(8,128)S(1)}, u32[]{:S(2)}, u32[]{:S(2)}) %all-to-all-start.5) | async-done | bytes 294944 | tf_op jit(solution)/shard_map/all_to_all | solution.py:537
  274.6 4.9 %finish.1 = (bf16[32,32,512]{2,1,0:T(8,128)(2,1)}, bf16[32,32,512]{2,1,0:T(8,128)(2,1)}) custom-call(s32[32]{0:T(128)} %fusion.7.pick_ref, bf16[32,128,512]{2,1,0:T(8,128)(2,1)} %bitcast.50, bf16[32,128,512]{2,1,0:T(8,128)(2,1)} %bitcast.51, bf16[32,128,512]{2,1,0:T(8,128)(2,1)} %bitcast.52, bf16[32,128,512]{2,1,0:T(8,128)(2,1)} %bitcast.53, ...), custom_call_target="tpu_custom_call" | custom-call | flops 134217728 | bytes 8388608 | tf_op jit(solution)/shard_map/finish/pallas_call | solution.py:516
  (117 shorter events, 47.2 us)
Async XLA Ops:
  8.8 65.4 %copy-start.27 = (bf16[32,3,256]{2,0,1:T(8,128)(2,1)S(1)}, bf16[32,3,256]{2,0,1:T(8,128)(2,1)}, u32[]{:S(2)}) copy-start(bf16[32,3,256]{2,0,1:T(8,128)(2,1)} %param.34) | copy-start | bytes 147460
  54.2 44.7 %all-to-all-start.2 = ((bf16[64,32,256]{2,1,0:T(8,128)(2,1)}), bf16[64,32,256]{2,1,0:T(8,128)(2,1)}, u32[]{:S(2)}, u32[]{:S(2)}) async-start(bf16[64,32,256]{2,1,0:T(8,128)(2,1)} %get-tuple-element.41), calls=%async_computation.2 | async-start | bytes 2097152 | tf_op jit(solution)/shard_map/all_to_all | solution.py:537
  61.2 7.7 %collective-permute-start.11 = (bf16[32,8,256]{2,1,0:T(8,128)(2,1)S(1)}, bf16[32,8,256]{2,1,0:T(8,128)(2,1)S(1)}, u32[]{:S(2)}, u32[]{:S(2)}) collective-permute-start(bf16[32,8,256]{2,1,0:T(8,128)(2,1)S(1)} %slice_bitcast_fusion.refs_0_), channel_id=1, source_target_pairs={{0,32},{32,64},{64,96},{96,128},{128,160},{160,192},{192,224},{224... | collective-permute-start | bytes 393224 | tf_op jit(solution)/shard_map/ppermute | solution.py:585
  61.3 9.0 %collective-permute-start.12 = (bf16[32,8,256]{2,1,0:T(8,128)(2,1)S(1)}, bf16[32,8,256]{2,1,0:T(8,128)(2,1)S(1)}, u32[]{:S(2)}, u32[]{:S(2)}) collective-permute-start(bf16[32,8,256]{2,1,0:T(8,128)(2,1)S(1)} %slice_bitcast_fusion.refs_0_), channel_id=1, source_target_pairs={{0,64},{32,96},{64,128},{96,160},{128,192},{160,224},{192,0},{224,... | collective-permute-start | bytes 393224 | tf_op jit(solution)/shard_map/ppermute | solution.py:585
  63.0 117.7 %copy-start.7 = (bf16[128,512]{1,0:T(8,128)(2,1)}, bf16[128,512]{1,0:T(8,128)(2,1)S(1)}, u32[]{:S(2)}) copy-start(bf16[128,512]{1,0:T(8,128)(2,1)S(1)} %pad_maximum_fusion.refs_0_) | copy-start | bytes 393220
  63.0 12.6 %collective-permute-start.13 = (bf16[32,8,256]{2,1,0:T(8,128)(2,1)S(1)}, bf16[32,8,256]{2,1,0:T(8,128)(2,1)S(1)}, u32[]{:S(2)}, u32[]{:S(2)}) collective-permute-start(bf16[32,8,256]{2,1,0:T(8,128)(2,1)S(1)} %slice_bitcast_fusion.refs_0_), channel_id=1, source_target_pairs={{0,96},{32,128},{64,160},{96,192},{128,224},{160,0},{192,32},{224,... | collective-permute-start | bytes 393224 | tf_op jit(solution)/shard_map/ppermute | solution.py:585
  65.2 10.5 %collective-permute-start.14 = (bf16[32,8,256]{2,1,0:T(8,128)(2,1)S(1)}, bf16[32,8,256]{2,1,0:T(8,128)(2,1)S(1)}, u32[]{:S(2)}, u32[]{:S(2)}) collective-permute-start(bf16[32,8,256]{2,1,0:T(8,128)(2,1)S(1)} %slice_bitcast_fusion.refs_0_), channel_id=1, source_target_pairs={{0,128},{32,160},{64,192},{96,224},{128,0},{160,32},{192,64},{224,... | collective-permute-start | bytes 393224 | tf_op jit(solution)/shard_map/ppermute | solution.py:585
  67.1 8.7 %collective-permute-start.15 = (bf16[32,8,256]{2,1,0:T(8,128)(2,1)S(1)}, bf16[32,8,256]{2,1,0:T(8,128)(2,1)S(1)}, u32[]{:S(2)}, u32[]{:S(2)}) collective-permute-start(bf16[32,8,256]{2,1,0:T(8,128)(2,1)S(1)} %slice_bitcast_fusion.refs_0_), channel_id=1, source_target_pairs={{0,160},{32,192},{64,224},{96,0},{128,32},{160,64},{192,96},{224,1... | collective-permute-start | bytes 393224 | tf_op jit(solution)/shard_map/ppermute | solution.py:585
  68.9 8.3 %collective-permute-start.16 = (bf16[32,8,256]{2,1,0:T(8,128)(2,1)S(1)}, bf16[32,8,256]{2,1,0:T(8,128)(2,1)S(1)}, u32[]{:S(2)}, u32[]{:S(2)}) collective-permute-start(bf16[32,8,256]{2,1,0:T(8,128)(2,1)S(1)} %slice_bitcast_fusion.refs_0_), channel_id=1, source_target_pairs={{0,192},{32,224},{64,0},{96,32},{128,64},{160,96},{192,128},{224,1... | collective-permute-start | bytes 393224 | tf_op jit(solution)/shard_map/ppermute | solution.py:585
  70.3 7.4 %collective-permute-start.17 = (bf16[32,8,256]{2,1,0:T(8,128)(2,1)S(1)}, bf16[32,8,256]{2,1,0:T(8,128)(2,1)S(1)}, u32[]{:S(2)}, u32[]{:S(2)}) collective-permute-start(bf16[32,8,256]{2,1,0:T(8,128)(2,1)S(1)} %slice_bitcast_fusion.refs_0_), channel_id=1, source_target_pairs={{0,224},{32,0},{64,32},{96,64},{128,96},{160,128},{192,160},{224,1... | collective-permute-start | bytes 393224 | tf_op jit(solution)/shard_map/ppermute | solution.py:585
  99.0 38.5 %all-to-all-start.1 = ((bf16[64,32,256]{2,1,0:T(8,128)(2,1)}), bf16[64,32,256]{2,1,0:T(8,128)(2,1)S(1)}, u32[]{:S(2)}, u32[]{:S(2)}) async-start(bf16[64,32,256]{2,1,0:T(8,128)(2,1)} %get-tuple-element.39), calls=%async_computation.1 | async-start | bytes 2097152 | tf_op jit(solution)/shard_map/all_to_all | solution.py:537
  137.4 106.4 %all-to-all-start.3 = ((bf16[64,32,256]{2,1,0:T(8,128)(2,1)}), bf16[64,32,256]{2,1,0:T(8,128)(2,1)}, u32[]{:S(2)}, u32[]{:S(2)}) async-start(bf16[64,32,256]{2,1,0:T(8,128)(2,1)} %get-tuple-element.44), calls=%async_computation.3 | async-start | bytes 2097152 | tf_op jit(solution)/shard_map/all_to_all | solution.py:537
  143.7 29.9 %collective-permute-start = (bf16[128,512]{1,0:T(8,128)(2,1)S(1)}, bf16[128,512]{1,0:T(8,128)(2,1)S(1)}, u32[]{:S(2)}, u32[]{:S(2)}) collective-permute-start(bf16[128,512]{1,0:T(8,128)(2,1)S(1)} %pad_maximum_fusion.refs_0_), channel_id=1, source_target_pairs={{0,4},{4,8},{8,12},{12,16},{16,20},{20,24},{24,28},{28,0},{1,5},{5... | collective-permute-start | bytes 393224 | tf_op jit(solution)/shard_map/ppermute | solution.py:585
  145.5 35.1 %collective-permute-start.1 = (bf16[128,512]{1,0:T(8,128)(2,1)S(1)}, bf16[128,512]{1,0:T(8,128)(2,1)S(1)}, u32[]{:S(2)}, u32[]{:S(2)}) collective-permute-start(bf16[128,512]{1,0:T(8,128)(2,1)S(1)} %pad_maximum_fusion.refs_0_), channel_id=1, source_target_pairs={{0,8},{4,12},{8,16},{12,20},{16,24},{20,28},{24,0},{28,4},{1,9},{5... | collective-permute-start | bytes 393224 | tf_op jit(solution)/shard_map/ppermute | solution.py:585
  147.8 39.5 %collective-permute-start.2 = (bf16[128,512]{1,0:T(8,128)(2,1)S(1)}, bf16[128,512]{1,0:T(8,128)(2,1)S(1)}, u32[]{:S(2)}, u32[]{:S(2)}) collective-permute-start(bf16[128,512]{1,0:T(8,128)(2,1)S(1)} %pad_maximum_fusion.refs_0_), channel_id=1, source_target_pairs={{0,12},{4,16},{8,20},{12,24},{16,28},{20,0},{24,4},{28,8},{1,13},{... | collective-permute-start | bytes 393224 | tf_op jit(solution)/shard_map/ppermute | solution.py:585
  150.5 41.4 %collective-permute-start.3 = (bf16[128,512]{1,0:T(8,128)(2,1)S(1)}, bf16[128,512]{1,0:T(8,128)(2,1)S(1)}, u32[]{:S(2)}, u32[]{:S(2)}) collective-permute-start(bf16[128,512]{1,0:T(8,128)(2,1)S(1)} %pad_maximum_fusion.refs_0_), channel_id=1, source_target_pairs={{0,16},{4,20},{8,24},{12,28},{16,0},{20,4},{24,8},{28,12},{1,17},{... | collective-permute-start | bytes 393224 | tf_op jit(solution)/shard_map/ppermute | solution.py:585
  152.9 39.0 %collective-permute-start.4 = (bf16[128,512]{1,0:T(8,128)(2,1)S(1)}, bf16[128,512]{1,0:T(8,128)(2,1)S(1)}, u32[]{:S(2)}, u32[]{:S(2)}) collective-permute-start(bf16[128,512]{1,0:T(8,128)(2,1)S(1)} %pad_maximum_fusion.refs_0_), channel_id=1, source_target_pairs={{0,20},{4,24},{8,28},{12,0},{16,4},{20,8},{24,12},{28,16},{1,21},{... | collective-permute-start | bytes 393224 | tf_op jit(solution)/shard_map/ppermute | solution.py:585
  173.7 18.2 %collective-permute-start.5 = (bf16[128,512]{1,0:T(8,128)(2,1)S(1)}, bf16[128,512]{1,0:T(8,128)(2,1)S(1)}, u32[]{:S(2)}, u32[]{:S(2)}) collective-permute-start(bf16[128,512]{1,0:T(8,128)(2,1)S(1)} %pad_maximum_fusion.refs_0_), channel_id=1, source_target_pairs={{0,24},{4,28},{8,0},{12,4},{16,8},{20,12},{24,16},{28,20},{1,25},{... | collective-permute-start | bytes 393224 | tf_op jit(solution)/shard_map/ppermute | solution.py:585
  180.6 11.3 %collective-permute-start.6 = (bf16[128,512]{1,0:T(8,128)(2,1)S(1)}, bf16[128,512]{1,0:T(8,128)(2,1)S(1)}, u32[]{:S(2)}, u32[]{:S(2)}) collective-permute-start(bf16[128,512]{1,0:T(8,128)(2,1)S(1)} %pad_maximum_fusion.refs_0_), channel_id=1, source_target_pairs={{0,28},{4,0},{8,4},{12,8},{16,12},{20,16},{24,20},{28,24},{1,29},{... | collective-permute-start | bytes 393224 | tf_op jit(solution)/shard_map/ppermute | solution.py:585
  195.4 24.7 %collective-permute-start.8 = (bf16[8,128,512]{2,1,0:T(8,128)(2,1)}, bf16[8,128,512]{2,1,0:T(8,128)(2,1)S(1)}, u32[]{:S(2)}, u32[]{:S(2)}) collective-permute-start(bf16[8,128,512]{2,1,0:T(8,128)(2,1)} %shard_map.227.refs_0_), channel_id=1, source_target_pairs={{0,3},{1,0},{2,1},{3,2},{4,7},{5,4},{6,5},{7,6},{8,11},{9,8},{10,9... | collective-permute-start | bytes 3145736 | tf_op jit(solution)/shard_map/ppermute | solution.py:585
  196.0 25.9 %collective-permute-start.7 = (bf16[8,128,512]{2,1,0:T(8,128)(2,1)}, bf16[8,128,512]{2,1,0:T(8,128)(2,1)S(1)}, u32[]{:S(2)}, u32[]{:S(2)}) collective-permute-start(bf16[8,128,512]{2,1,0:T(8,128)(2,1)} %shard_map.227.refs_0_), channel_id=1, source_target_pairs={{0,1},{1,2},{2,3},{3,0},{4,5},{5,6},{6,7},{7,4},{8,9},{9,10},{10,1... | collective-permute-start | bytes 3145736 | tf_op jit(solution)/shard_map/ppermute | solution.py:585
  221.2 12.5 %collective-permute-start.10 = (bf16[8,64,512]{2,1,0:T(8,128)(2,1)S(1)}, bf16[8,64,512]{2,1,0:T(8,128)(2,1)}, u32[]{:S(2)}, u32[]{:S(2)}) collective-permute-start(bf16[8,64,512]{2,1,0:T(8,128)(2,1)S(1)} %slice.13), channel_id=1, source_target_pairs={{0,3},{1,0},{2,1},{3,2},{4,7},{5,4},{6,5},{7,6},{8,11},{9,8},{10,9... | collective-permute-start | bytes 1572872 | tf_op jit(solution)/shard_map/ppermute | solution.py:585
  222.0 14.0 %collective-permute-start.9 = (bf16[8,64,512]{2,1,0:T(8,128)(2,1)S(1)}, bf16[8,64,512]{2,1,0:T(8,128)(2,1)}, u32[]{:S(2)}, u32[]{:S(2)}) collective-permute-start(bf16[8,64,512]{2,1,0:T(8,128)(2,1)S(1)} %slice.12), channel_id=1, source_target_pairs={{0,1},{1,2},{2,3},{3,0},{4,5},{5,6},{6,7},{7,4},{8,9},{9,10},{10,1... | collective-permute-start | bytes 1572872 | tf_op jit(solution)/shard_map/ppermute | solution.py:585
  262.6 11.2 %all-to-all-start.5 = ((f32[8,72,128]{2,1,0:T(8,128)}), f32[8,72,128]{2,1,0:T(8,128)S(1)}, u32[]{:S(2)}, u32[]{:S(2)}) async-start(f32[8,72,128]{2,1,0:T(8,128)} %broadcast_in_dim.80), calls=%async_computation.5 | async-start | bytes 589824 | tf_op jit(solution)/shard_map/all_to_all | solution.py:537
  (28 other events, 462.0 us)
where the time goes:
time: 284 us; the launch traced here: 280 us
  waiting for transfers between devices  98.1 us (35%)
  blocking collectives  58.9 us (21%)
  starting transfers between devices  54.8 us (19%)
  Pallas kernels  51.5 us (18%)
  local copies, waits for them, and re-layouts  9.99 us (4%)
  other arithmetic  5.15 us (2%)
    ppermute x18, waiting for transfers between devices, shift(): return lax.ppermute(value, axis, pairs)  71.3 us
    all_to_all x2, blocking collectives, exchange(): lax.all_to_all(value, axis, split_axis=0, concat_axis=0, tiled=True, axis...  58.9 us
    ppermute x18, starting transfers between devices, shift(): return lax.ppermute(value, axis, pairs)  29 us
    all_to_all x4, waiting for transfers between devices, exchange(): lax.all_to_all(value, axis, split_axis=0, concat_axis=0, tiled=True, axis...  26.8 us
    all_to_all x4, starting transfers between devices, exchange(): lax.all_to_all(value, axis, split_axis=0, concat_axis=0, tiled=True, axis...  25.8 us
    pallas_call x2, Pallas kernels, mix(): pl.pallas_call(body, out_shape=[jax.ShapeDtypeStruct((slot_total, tokens,...  16.5 us
    pallas_call x1, Pallas kernels, prepare(): pl.pallas_call(body, out_shape=[jax.ShapeDtypeStruct((sessions, tokens, 2...  9.99 us
    pallas_call x2, Pallas kernels, gate_rows(): pl.pallas_call(body, out_shape=[jax.ShapeDtypeStruct((sessions // BLOCK *...  9.12 us
  transfers between devices with their start and end apart: 22, of which 12 were waited for; matrix products, arithmetic and copies ran while one was open for 2% of the time, Pallas kernels for 14%

commit v1 on v0

--- a/solution.py
+++ b/solution.py
@@ -56,7 +56,7 @@
     return silu(summed)
 
 
-def pack(slots, rank_here, map_slice, step_rows, rows_in, slot_total):
+def pack(slots, rank_here, map_slice, steps, rows_in, slot_total):
     sessions, tokens, channels = rows_in.shape
     _, group_tokens, map_width = map_slice.shape
     width = channels // CHUNKS
@@ -64,7 +64,7 @@
 
     def body(slot_ref, rank_ref, map_ref, step_ref, in_ref, *rest):
         outs = rest[:CHUNKS]
-        small_sc, step_sc, sems, small_sem = rest[CHUNKS:]
+        small_sc, row_sc, step_sc, sems, small_sem = rest[CHUNKS:]
 
         def copies(q):
             slot = slot_ref[q]
@@ -80,10 +80,13 @@
         for q in range(sessions):
             for copy in copies(q):
                 copy.start()
+        heads = step_ref.shape[1]
+        raw = step_ref[...].astype(F32)
+        row_sc[...] = jnp.concatenate([raw[:, h, :] for h in range(heads)], axis=1)
         for q in range(sessions):
             home = slot_ref[q] // PAIR
             rank = slot_ref[q] % PAIR
-            step_sc[home, pl.ds(rank, 1), :] = step_ref[q : q + 1, :]
+            step_sc[home, pl.ds(rank, 1), :] = row_sc[q : q + 1, :]
 
             @pl.when(rank == rank_ref[0])
             def _():
@@ -116,6 +119,7 @@
         out_specs=[pl.BlockSpec(memory_space=pl.ANY)] * CHUNKS,
         scratch_shapes=[
             pltpu.VMEM((slot_total // PAIR, PAIR, extra, map_width), BF16),
+            pltpu.VMEM((sessions, map_width), F32),
             pltpu.VMEM((slot_total // PAIR, 8, map_width), F32),
             pltpu.SemaphoreType.DMA((CHUNKS * sessions,)),
             pltpu.SemaphoreType.DMA((slot_total // PAIR,)),
@@ -123,7 +127,7 @@
         compiler_params=params(),
         cost_estimate=cost(0, 4 << 20),
         name="pack",
-    )(slots, rank_here, map_slice, step_rows, rows_in)
+    )(slots, rank_here, map_slice, steps, rows_in)
 
 
 def prepare(slots, lens, maps, fresh, map_window, state, map_kernel, map_bias, bias, decay):
@@ -630,7 +634,6 @@
     session_adapter_index,
 ):
     sessions, tokens, channels = channel_rows_in.shape
-    heads = step_size_input.shape[1]
     rows = lax.axis_size("row")
     sections = lax.axis_size("section")
     row = lax.axis_index("row")
@@ -659,9 +662,8 @@
     map_slice = lax.dynamic_slice_in_dim(
         map_input_rows, section % side * group_tokens, group_tokens, axis=1
     )
-    step_rows = step_size_input.reshape(sessions, heads * tokens).astype(F32)
     sent = pack(
-        serve_slots, (section // side).reshape(1), map_slice, step_rows, channel_rows_in, rows * PAIR
+        serve_slots, (section // side).reshape(1), map_slice, step_size_input, channel_rows_in, rows * PAIR
     )
     fresh = []
     for k in range(CHUNKS):

time: 284 us -> 283 us (level)
  no operation moved by 1% of the time
where the time goes in v1:
time: 283 us; the launch traced here: 278 us
  waiting for transfers between devices  98.1 us (35%)
  blocking collectives  58.9 us (21%)
  starting transfers between devices  54.8 us (19%)
  Pallas kernels  51.5 us (18%)
  local copies, waits for them, and re-layouts  8.43 us (3%)
  other arithmetic  5.15 us (2%)
    ppermute x18, waiting for transfers between devices, shift(): return lax.ppermute(value, axis, pairs)  71.3 us
    all_to_all x2, blocking collectives, exchange(): lax.all_to_all(value, axis, split_axis=0, concat_axis=0, tiled=True, axis...  58.9 us
    ppermute x18, starting transfers between devices, shift(): return lax.ppermute(value, axis, pairs)  29 us
    all_to_all x4, waiting for transfers between devices, exchange(): lax.all_to_all(value, axis, split_axis=0, concat_axis=0, tiled=True, axis...  26.8 us
    all_to_all x4, starting transfers between devices, exchange(): lax.all_to_all(value, axis, split_axis=0, concat_axis=0, tiled=True, axis...  25.8 us
    pallas_call x2, Pallas kernels, mix(): pl.pallas_call(body, out_shape=[jax.ShapeDtypeStruct((slot_total, tokens,...  16.5 us
    pallas_call x1, Pallas kernels, prepare(): pl.pallas_call(body, out_shape=[jax.ShapeDtypeStruct((sessions, tokens, 2...  10 us
    pallas_call x2, Pallas kernels, gate_rows(): pl.pallas_call(body, out_shape=[jax.ShapeDtypeStruct((sessions // BLOCK *...  9.12 us
  transfers between devices with their start and end apart: 22, of which 12 were waited for; matrix products, arithmetic and copies ran while one was open for 2% of the time, Pallas kernels for 14%

profile of v1, /device:TPU:2, one launch (start us, length us, event | category | flops | bytes accessed | tf_op | source)
XLA Modules:
  0.0 278.1 jit_solution(6150023473709631010)
XLA Ops:
  3.7 3.5 %pack.1 = (bf16[64,40,256]{2,1,0:T(8,128)(2,1)}, bf16[64,32,256]{2,1,0:T(8,128)(2,1)}) custom-call(s32[32]{0:T(128)} %multiply_add_fusion.slot_ref, s32[1]{0:T(128)} %bitcast.5.rank_ref, bf16[32,8,256]{2,1,0:T(8,128)(2,1)} %constant_dynamic-slice_fusion.map_ref, bf16[32,8,32]{2,1,0:T(8,128)(2,1)} %step_ref.1, bf16[32,32,512]{2,1,0:T(8,128)(2,1)} %in_ref.1), custom_call_target="tpu_custom_call" | custom-call | bytes 4194304 | tf_op jit(solution)/shard_map/pack/pallas_call | solution.py:112
  7.2 45.4 %all_to_all.37.refs_8_.refs_0_.refs_1_.refs_2_.refs_3_.refs_4_.refs_5_.refs_6_.refs_7_ = bf16[64,40,256]{2,1,0:T(8,128)(2,1)S(1)} all-to-all(bf16[64,40,256]{2,1,0:T(8,128)(2,1)} %get-tuple-element.33), channel_id=1, replica_groups=mesh['section'=8,'row'=32] {'row'}, dimensions={0} | all-to-all | bytes 2621440 | tf_op jit(solution)/shard_map/all_to_all | solution.py:541
  52.7 6.2 %all-to-all-start.2 = ((bf16[64,32,256]{2,1,0:T(8,128)(2,1)}), bf16[64,32,256]{2,1,0:T(8,128)(2,1)}, u32[]{:S(2)}, u32[]{:S(2)}) async-start(bf16[64,32,256]{2,1,0:T(8,128)(2,1)} %get-tuple-element.41), calls=%async_computation.2 | async-start | bytes 2097152 | tf_op jit(solution)/shard_map/all_to_all | solution.py:541
  79.1 10.0 %prepare.1 = (bf16[32,32,512]{2,1,0:T(8,128)(2,1)}, f32[32,32,512]{2,1,0:T(8,128)}, f32[32,32,512]{2,1,0:T(8,128)}, bf16[32,96,128]{2,1,0:T(8,128)(2,1)}, f32[32...) custom-call(s32[32]{0:T(128)} %get-tuple-element.31.slot_ref, s32[32]{0:T(128)} %get-tuple-element.32.len_ref, ...), custom_call_target="tpu_custom_call" | custom-call | flops 1073741824 | bytes 16777216 | tf_op jit(solution)/shard_map/prepare/pallas_call | solution.py:260
  89.1 8.3 %shard_map.230 = (bf16[64,32,256]{2,1,0:T(8,128)(2,1)}, bf16[32,8,64,128]{3,2,1,0:T(8,128)(2,1)}, bf16[32,3,512]{2,1,0:T(4,128)(2,1)}) custom-call(s32[32]{0:T(128)} %get-tuple-element.31.slot_ref, s32[32]{0:T(128)} %get-tuple-element.32.len_ref, bf16[64,40,256]{2,1,0:T(8,128)(2,1)} %copy-done.2, bf16[64,40,256]{2,1,0:T(8,128)(2,1)} %copy-done.2, ...), custom_call_target="tpu_custom_call" | custom-call | flops 536870912 | bytes 16777216 | tf_op jit(solution)/shard_map/pallas_call | solution.py:391
  97.4 9.9 %all-to-all-start.1 = ((bf16[64,32,256]{2,1,0:T(8,128)(2,1)}), bf16[64,32,256]{2,1,0:T(8,128)(2,1)S(1)}, u32[]{:S(2)}, u32[]{:S(2)}) async-start(bf16[64,32,256]{2,1,0:T(8,128)(2,1)} %get-tuple-element.39), calls=%async_computation.1 | async-start | bytes 2097152 | tf_op jit(solution)/shard_map/all_to_all | solution.py:541
  107.3 8.3 %shard_map.232 = (bf16[64,32,256]{2,1,0:T(8,128)(2,1)}, bf16[32,8,64,128]{3,2,1,0:T(8,128)(2,1)}, bf16[32,3,512]{2,1,0:T(4,128)(2,1)}) custom-call(s32[32]{0:T(128)} %get-tuple-element.31.slot_ref, s32[32]{0:T(128)} %get-tuple-element.32.len_ref, ...), custom_call_target="tpu_custom_call", output_to_operand_aliasing={{1}: (20, {}), {2}: (21, {})} | custom-call | flops 536870912 | bytes 16777216 | tf_op jit(solution)/shard_map/pallas_call | solution.py:391
  115.6 20.3 %all-to-all-done.1.refs_0_.refs_1_.refs_2_.refs_3_.refs_4_.refs_5_.refs_6_.refs_7_.refs_8_.refs_9_.refs_10_.refs_11_.refs_12_.refs_13_.refs_14_.refs_15_ = bf16[64,32,256]{2,1,0:T(8,128)(2,1)S(1)} async-done(((bf16[64,32,256]{2,1,0:T(8,128)(2,1)}), bf16[64,32,256]{2,1,0:T(8,128)(2,1)S(1)}, u32[]{:S(2)}, u32[]{:S(2)}) %all-to-all-start.1) | async-done | bytes 1048608 | tf_op jit(solution)/shard_map/all_to_all | solution.py:541
  135.9 6.3 %all-to-all-start.3 = ((bf16[64,32,256]{2,1,0:T(8,128)(2,1)}), bf16[64,32,256]{2,1,0:T(8,128)(2,1)}, u32[]{:S(2)}, u32[]{:S(2)}) async-start(bf16[64,32,256]{2,1,0:T(8,128)(2,1)} %get-tuple-element.44), calls=%async_computation.3 | async-start | bytes 2097152 | tf_op jit(solution)/shard_map/all_to_all | solution.py:541
  146.3 2.7 collective-permute-start.2
  151.3 2.7 collective-permute-start.4
  154.1 18.1 %collective-permute-done.refs_1_ = bf16[128,512]{1,0:T(8,128)(2,1)S(1)} collective-permute-done((bf16[128,512]{1,0:T(8,128)(2,1)S(1)}, bf16[128,512]{1,0:T(8,128)(2,1)S(1)}, u32[]{:S(2)}, u32[]{:S(2)}) %collective-permute-start) | collective-permute-done | bytes 131104 | tf_op jit(solution)/shard_map/ppermute | solution.py:589
  173.8 5.3 %collective-permute-done.1.refs_2_ = bf16[128,512]{1,0:T(8,128)(2,1)S(1)} collective-permute-done((bf16[128,512]{1,0:T(8,128)(2,1)S(1)}, bf16[128,512]{1,0:T(8,128)(2,1)S(1)}, u32[]{:S(2)}, u32[]{:S(2)}) %collective-permute-start.1) | collective-permute-done | bytes 131104 | tf_op jit(solution)/shard_map/ppermute | solution.py:589
  179.5 6.3 %collective-permute-done.2.refs_3_ = bf16[128,512]{1,0:T(8,128)(2,1)S(1)} collective-permute-done((bf16[128,512]{1,0:T(8,128)(2,1)S(1)}, bf16[128,512]{1,0:T(8,128)(2,1)S(1)}, u32[]{:S(2)}, u32[]{:S(2)}) %collective-permute-start.2) | collective-permute-done | bytes 131104 | tf_op jit(solution)/shard_map/ppermute | solution.py:589
  185.8 4.6 %collective-permute-done.3.refs_4_ = bf16[128,512]{1,0:T(8,128)(2,1)S(1)} collective-permute-done((bf16[128,512]{1,0:T(8,128)(2,1)S(1)}, bf16[128,512]{1,0:T(8,128)(2,1)S(1)}, u32[]{:S(2)}, u32[]{:S(2)}) %collective-permute-start.3) | collective-permute-done | bytes 131104 | tf_op jit(solution)/shard_map/ppermute | solution.py:589
  196.0 22.6 %collective-permute-done.8.refs_2_ = bf16[8,128,512]{2,1,0:T(8,128)(2,1)S(1)} collective-permute-done((bf16[8,128,512]{2,1,0:T(8,128)(2,1)}, bf16[8,128,512]{2,1,0:T(8,128)(2,1)S(1)}, u32[]{:S(2)}, u32[]{:S(2)}) %collective-permute-start.8) | collective-permute-done | bytes 1048608 | tf_op jit(solution)/shard_map/ppermute | solution.py:589
  221.9 10.3 %collective-permute-done.10.refs_4_ = bf16[8,64,512]{2,1,0:T(8,128)(2,1)} collective-permute-done((bf16[8,64,512]{2,1,0:T(8,128)(2,1)S(1)}, bf16[8,64,512]{2,1,0:T(8,128)(2,1)}, u32[]{:S(2)}, u32[]{:S(2)}) %collective-permute-start.10) | collective-permute-done | bytes 524320 | tf_op jit(solution)/shard_map/ppermute | solution.py:589
  234.4 3.3 %shard_map.228 = bf16[4,8,128,512]{3,2,1,0:T(8,128)(2,1)} custom-call(s32[1]{0:T(128)} %bitcast.2.base_ref, bf16[8,128,512]{2,1,0:T(8,128)(2,1)} %shard_map.227.refs_0_, bf16[8,128,512]{2,1,0:T(8,128)(2,1)} %copy-done.4, bf16[8,128,512]{2,1,0:T(8,128)(2,1)} %copy-done.3, bf16[8,64,512]{2,1,0:T(8,128)(2,1)} %collective-permute-done.9.refs_3_, ...), custom_call_target="tpu_custom_call" | custom-call | bytes 8388608 | tf_op jit(solution)/shard_map/pallas_call | solution.py:574
  237.7 4.5 %shard_map.231 = (f32[576,128]{1,0:T(8,128)}, f32[32,32,256]{2,1,0:T(8,128)}) custom-call(s32[32]{0:T(128)} %multiply_add_fusion.slot_ref, s32[32]{0:T(128)} %fusion.7.pick_ref, bf16[64,32,256]{2,1,0:T(8,128)(2,1)} %copy-done.1, bf16[64,32,256]{2,1,0:T(8,128)(2,1)} %copy-done.1, bf16[64,32,256]{2,1,0:T(8,128)(2,1)} %copy-done.1, ...), custom_call_target="tpu_custom_call" | custom-call | flops 134217728 | bytes 8388608 | tf_op jit(solution)/shard_map/pallas_call | solution.py:468
  242.3 4.6 %shard_map.233 = (f32[576,128]{1,0:T(8,128)}, f32[32,32,256]{2,1,0:T(8,128)}) custom-call(s32[32]{0:T(128)} %multiply_add_fusion.slot_ref, s32[32]{0:T(128)} %fusion.7.pick_ref, bf16[64,32,256]{2,1,0:T(8,128)(2,1)} %all-to-all-done.3.refs_0_.refs_1_.refs_2_.refs_3_.refs_4_.refs_5_.refs_6_.refs_7_.refs_8_.refs_9_.refs_10_.refs_11_.refs_12_.refs_13_.refs_14_.refs_15_, ...), custom_call_target="tpu_custom_call" | custom-call | flops 134217728 | bytes 8388608 | tf_op jit(solution)/shard_map/pallas_call | solution.py:468
  246.9 13.4 %all_to_all.38 = f32[8,72,128]{2,1,0:T(8,128)S(1)} all-to-all(f32[8,72,128]{2,1,0:T(8,128)} %bitcast.76), channel_id=1, replica_groups=mesh['section'=8,'row'=32] {'section'}, dimensions={0} | all-to-all | bytes 589824 | tf_op jit(solution)/shard_map/all_to_all | solution.py:541
  261.1 3.4 %all-to-all-start.5 = ((f32[8,72,128]{2,1,0:T(8,128)}), f32[8,72,128]{2,1,0:T(8,128)S(1)}, u32[]{:S(2)}, u32[]{:S(2)}) async-start(f32[8,72,128]{2,1,0:T(8,128)} %broadcast_in_dim.80), calls=%async_computation.5 | async-start | bytes 589824 | tf_op jit(solution)/shard_map/all_to_all | solution.py:541
  265.8 6.5 %all-to-all-done.5 = f32[8,72,128]{2,1,0:T(8,128)S(1)} async-done(((f32[8,72,128]{2,1,0:T(8,128)}), f32[8,72,128]{2,1,0:T(8,128)S(1)}, u32[]{:S(2)}, u32[]{:S(2)}) %all-to-all-start.5) | async-done | bytes 294944 | tf_op jit(solution)/shard_map/all_to_all | solution.py:541
  273.0 4.9 %finish.1 = (bf16[32,32,512]{2,1,0:T(8,128)(2,1)}, bf16[32,32,512]{2,1,0:T(8,128)(2,1)}) custom-call(s32[32]{0:T(128)} %fusion.7.pick_ref, bf16[32,128,512]{2,1,0:T(8,128)(2,1)} %bitcast.50, bf16[32,128,512]{2,1,0:T(8,128)(2,1)} %bitcast.51, bf16[32,128,512]{2,1,0:T(8,128)(2,1)} %bitcast.52, bf16[32,128,512]{2,1,0:T(8,128)(2,1)} %bitcast.53, ...), custom_call_target="tpu_custom_call" | custom-call | flops 134217728 | bytes 8388608 | tf_op jit(solution)/shard_map/finish/pallas_call | solution.py:520
  (116 shorter events, 45.6 us)
Async XLA Ops:
  7.2 65.4 %copy-start.27 = (bf16[32,3,256]{2,0,1:T(8,128)(2,1)S(1)}, bf16[32,3,256]{2,0,1:T(8,128)(2,1)}, u32[]{:S(2)}) copy-start(bf16[32,3,256]{2,0,1:T(8,128)(2,1)} %param.34) | copy-start | bytes 147460
  52.7 44.7 %all-to-all-start.2 = ((bf16[64,32,256]{2,1,0:T(8,128)(2,1)}), bf16[64,32,256]{2,1,0:T(8,128)(2,1)}, u32[]{:S(2)}, u32[]{:S(2)}) async-start(bf16[64,32,256]{2,1,0:T(8,128)(2,1)} %get-tuple-element.41), calls=%async_computation.2 | async-start | bytes 2097152 | tf_op jit(solution)/shard_map/all_to_all | solution.py:541
  59.7 7.7 %collective-permute-start.11 = (bf16[32,8,256]{2,1,0:T(8,128)(2,1)S(1)}, bf16[32,8,256]{2,1,0:T(8,128)(2,1)S(1)}, u32[]{:S(2)}, u32[]{:S(2)}) collective-permute-start(bf16[32,8,256]{2,1,0:T(8,128)(2,1)S(1)} %slice_bitcast_fusion.refs_0_), channel_id=1, source_target_pairs={{0,32},{32,64},{64,96},{96,128},{128,160},{160,192},{192,224},{224... | collective-permute-start | bytes 393224 | tf_op jit(solution)/shard_map/ppermute | solution.py:589
  59.7 9.0 %collective-permute-start.12 = (bf16[32,8,256]{2,1,0:T(8,128)(2,1)S(1)}, bf16[32,8,256]{2,1,0:T(8,128)(2,1)S(1)}, u32[]{:S(2)}, u32[]{:S(2)}) collective-permute-start(bf16[32,8,256]{2,1,0:T(8,128)(2,1)S(1)} %slice_bitcast_fusion.refs_0_), channel_id=1, source_target_pairs={{0,64},{32,96},{64,128},{96,160},{128,192},{160,224},{192,0},{224,... | collective-permute-start | bytes 393224 | tf_op jit(solution)/shard_map/ppermute | solution.py:589
  61.4 117.7 %copy-start.7 = (bf16[128,512]{1,0:T(8,128)(2,1)}, bf16[128,512]{1,0:T(8,128)(2,1)S(1)}, u32[]{:S(2)}) copy-start(bf16[128,512]{1,0:T(8,128)(2,1)S(1)} %pad_maximum_fusion.refs_0_) | copy-start | bytes 393220
  61.4 12.6 %collective-permute-start.13 = (bf16[32,8,256]{2,1,0:T(8,128)(2,1)S(1)}, bf16[32,8,256]{2,1,0:T(8,128)(2,1)S(1)}, u32[]{:S(2)}, u32[]{:S(2)}) collective-permute-start(bf16[32,8,256]{2,1,0:T(8,128)(2,1)S(1)} %slice_bitcast_fusion.refs_0_), channel_id=1, source_target_pairs={{0,96},{32,128},{64,160},{96,192},{128,224},{160,0},{192,32},{224,... | collective-permute-start | bytes 393224 | tf_op jit(solution)/shard_map/ppermute | solution.py:589
  63.7 10.5 %collective-permute-start.14 = (bf16[32,8,256]{2,1,0:T(8,128)(2,1)S(1)}, bf16[32,8,256]{2,1,0:T(8,128)(2,1)S(1)}, u32[]{:S(2)}, u32[]{:S(2)}) collective-permute-start(bf16[32,8,256]{2,1,0:T(8,128)(2,1)S(1)} %slice_bitcast_fusion.refs_0_), channel_id=1, source_target_pairs={{0,128},{32,160},{64,192},{96,224},{128,0},{160,32},{192,64},{224,... | collective-permute-start | bytes 393224 | tf_op jit(solution)/shard_map/ppermute | solution.py:589
  65.5 8.7 %collective-permute-start.15 = (bf16[32,8,256]{2,1,0:T(8,128)(2,1)S(1)}, bf16[32,8,256]{2,1,0:T(8,128)(2,1)S(1)}, u32[]{:S(2)}, u32[]{:S(2)}) collective-permute-start(bf16[32,8,256]{2,1,0:T(8,128)(2,1)S(1)} %slice_bitcast_fusion.refs_0_), channel_id=1, source_target_pairs={{0,160},{32,192},{64,224},{96,0},{128,32},{160,64},{192,96},{224,1... | collective-permute-start | bytes 393224 | tf_op jit(solution)/shard_map/ppermute | solution.py:589
  67.4 8.3 %collective-permute-start.16 = (bf16[32,8,256]{2,1,0:T(8,128)(2,1)S(1)}, bf16[32,8,256]{2,1,0:T(8,128)(2,1)S(1)}, u32[]{:S(2)}, u32[]{:S(2)}) collective-permute-start(bf16[32,8,256]{2,1,0:T(8,128)(2,1)S(1)} %slice_bitcast_fusion.refs_0_), channel_id=1, source_target_pairs={{0,192},{32,224},{64,0},{96,32},{128,64},{160,96},{192,128},{224,1... | collective-permute-start | bytes 393224 | tf_op jit(solution)/shard_map/ppermute | solution.py:589
  68.7 7.4 %collective-permute-start.17 = (bf16[32,8,256]{2,1,0:T(8,128)(2,1)S(1)}, bf16[32,8,256]{2,1,0:T(8,128)(2,1)S(1)}, u32[]{:S(2)}, u32[]{:S(2)}) collective-permute-start(bf16[32,8,256]{2,1,0:T(8,128)(2,1)S(1)} %slice_bitcast_fusion.refs_0_), channel_id=1, source_target_pairs={{0,224},{32,0},{64,32},{96,64},{128,96},{160,128},{192,160},{224,1... | collective-permute-start | bytes 393224 | tf_op jit(solution)/shard_map/ppermute | solution.py:589
  97.4 38.5 %all-to-all-start.1 = ((bf16[64,32,256]{2,1,0:T(8,128)(2,1)}), bf16[64,32,256]{2,1,0:T(8,128)(2,1)S(1)}, u32[]{:S(2)}, u32[]{:S(2)}) async-start(bf16[64,32,256]{2,1,0:T(8,128)(2,1)} %get-tuple-element.39), calls=%async_computation.1 | async-start | bytes 2097152 | tf_op jit(solution)/shard_map/all_to_all | solution.py:541
  135.9 106.4 %all-to-all-start.3 = ((bf16[64,32,256]{2,1,0:T(8,128)(2,1)}), bf16[64,32,256]{2,1,0:T(8,128)(2,1)}, u32[]{:S(2)}, u32[]{:S(2)}) async-start(bf16[64,32,256]{2,1,0:T(8,128)(2,1)} %get-tuple-element.44), calls=%async_computation.3 | async-start | bytes 2097152 | tf_op jit(solution)/shard_map/all_to_all | solution.py:541
  142.2 29.9 %collective-permute-start = (bf16[128,512]{1,0:T(8,128)(2,1)S(1)}, bf16[128,512]{1,0:T(8,128)(2,1)S(1)}, u32[]{:S(2)}, u32[]{:S(2)}) collective-permute-start(bf16[128,512]{1,0:T(8,128)(2,1)S(1)} %pad_maximum_fusion.refs_0_), channel_id=1, source_target_pairs={{0,4},{4,8},{8,12},{12,16},{16,20},{20,24},{24,28},{28,0},{1,5},{5... | collective-permute-start | bytes 393224 | tf_op jit(solution)/shard_map/ppermute | solution.py:589
  143.9 35.1 %collective-permute-start.1 = (bf16[128,512]{1,0:T(8,128)(2,1)S(1)}, bf16[128,512]{1,0:T(8,128)(2,1)S(1)}, u32[]{:S(2)}, u32[]{:S(2)}) collective-permute-start(bf16[128,512]{1,0:T(8,128)(2,1)S(1)} %pad_maximum_fusion.refs_0_), channel_id=1, source_target_pairs={{0,8},{4,12},{8,16},{12,20},{16,24},{20,28},{24,0},{28,4},{1,9},{5... | collective-permute-start | bytes 393224 | tf_op jit(solution)/shard_map/ppermute | solution.py:589
  146.3 39.5 %collective-permute-start.2 = (bf16[128,512]{1,0:T(8,128)(2,1)S(1)}, bf16[128,512]{1,0:T(8,128)(2,1)S(1)}, u32[]{:S(2)}, u32[]{:S(2)}) collective-permute-start(bf16[128,512]{1,0:T(8,128)(2,1)S(1)} %pad_maximum_fusion.refs_0_), channel_id=1, source_target_pairs={{0,12},{4,16},{8,20},{12,24},{16,28},{20,0},{24,4},{28,8},{1,13},{... | collective-permute-start | bytes 393224 | tf_op jit(solution)/shard_map/ppermute | solution.py:589
  149.0 41.4 %collective-permute-start.3 = (bf16[128,512]{1,0:T(8,128)(2,1)S(1)}, bf16[128,512]{1,0:T(8,128)(2,1)S(1)}, u32[]{:S(2)}, u32[]{:S(2)}) collective-permute-start(bf16[128,512]{1,0:T(8,128)(2,1)S(1)} %pad_maximum_fusion.refs_0_), channel_id=1, source_target_pairs={{0,16},{4,20},{8,24},{12,28},{16,0},{20,4},{24,8},{28,12},{1,17},{... | collective-permute-start | bytes 393224 | tf_op jit(solution)/shard_map/ppermute | solution.py:589
  151.3 39.0 %collective-permute-start.4 = (bf16[128,512]{1,0:T(8,128)(2,1)S(1)}, bf16[128,512]{1,0:T(8,128)(2,1)S(1)}, u32[]{:S(2)}, u32[]{:S(2)}) collective-permute-start(bf16[128,512]{1,0:T(8,128)(2,1)S(1)} %pad_maximum_fusion.refs_0_), channel_id=1, source_target_pairs={{0,20},{4,24},{8,28},{12,0},{16,4},{20,8},{24,12},{28,16},{1,21},{... | collective-permute-start | bytes 393224 | tf_op jit(solution)/shard_map/ppermute | solution.py:589
  172.1 18.2 %collective-permute-start.5 = (bf16[128,512]{1,0:T(8,128)(2,1)S(1)}, bf16[128,512]{1,0:T(8,128)(2,1)S(1)}, u32[]{:S(2)}, u32[]{:S(2)}) collective-permute-start(bf16[128,512]{1,0:T(8,128)(2,1)S(1)} %pad_maximum_fusion.refs_0_), channel_id=1, source_target_pairs={{0,24},{4,28},{8,0},{12,4},{16,8},{20,12},{24,16},{28,20},{1,25},{... | collective-permute-start | bytes 393224 | tf_op jit(solution)/shard_map/ppermute | solution.py:589
  179.1 11.3 %collective-permute-start.6 = (bf16[128,512]{1,0:T(8,128)(2,1)S(1)}, bf16[128,512]{1,0:T(8,128)(2,1)S(1)}, u32[]{:S(2)}, u32[]{:S(2)}) collective-permute-start(bf16[128,512]{1,0:T(8,128)(2,1)S(1)} %pad_maximum_fusion.refs_0_), channel_id=1, source_target_pairs={{0,28},{4,0},{8,4},{12,8},{16,12},{20,16},{24,20},{28,24},{1,29},{... | collective-permute-start | bytes 393224 | tf_op jit(solution)/shard_map/ppermute | solution.py:589
  193.9 24.7 %collective-permute-start.8 = (bf16[8,128,512]{2,1,0:T(8,128)(2,1)}, bf16[8,128,512]{2,1,0:T(8,128)(2,1)S(1)}, u32[]{:S(2)}, u32[]{:S(2)}) collective-permute-start(bf16[8,128,512]{2,1,0:T(8,128)(2,1)} %shard_map.227.refs_0_), channel_id=1, source_target_pairs={{0,3},{1,0},{2,1},{3,2},{4,7},{5,4},{6,5},{7,6},{8,11},{9,8},{10,9... | collective-permute-start | bytes 3145736 | tf_op jit(solution)/shard_map/ppermute | solution.py:589
  194.4 25.9 %collective-permute-start.7 = (bf16[8,128,512]{2,1,0:T(8,128)(2,1)}, bf16[8,128,512]{2,1,0:T(8,128)(2,1)S(1)}, u32[]{:S(2)}, u32[]{:S(2)}) collective-permute-start(bf16[8,128,512]{2,1,0:T(8,128)(2,1)} %shard_map.227.refs_0_), channel_id=1, source_target_pairs={{0,1},{1,2},{2,3},{3,0},{4,5},{5,6},{6,7},{7,4},{8,9},{9,10},{10,1... | collective-permute-start | bytes 3145736 | tf_op jit(solution)/shard_map/ppermute | solution.py:589
  219.6 12.5 %collective-permute-start.10 = (bf16[8,64,512]{2,1,0:T(8,128)(2,1)S(1)}, bf16[8,64,512]{2,1,0:T(8,128)(2,1)}, u32[]{:S(2)}, u32[]{:S(2)}) collective-permute-start(bf16[8,64,512]{2,1,0:T(8,128)(2,1)S(1)} %slice.13), channel_id=1, source_target_pairs={{0,3},{1,0},{2,1},{3,2},{4,7},{5,4},{6,5},{7,6},{8,11},{9,8},{10,9... | collective-permute-start | bytes 1572872 | tf_op jit(solution)/shard_map/ppermute | solution.py:589
  220.4 14.0 %collective-permute-start.9 = (bf16[8,64,512]{2,1,0:T(8,128)(2,1)S(1)}, bf16[8,64,512]{2,1,0:T(8,128)(2,1)}, u32[]{:S(2)}, u32[]{:S(2)}) collective-permute-start(bf16[8,64,512]{2,1,0:T(8,128)(2,1)S(1)} %slice.12), channel_id=1, source_target_pairs={{0,1},{1,2},{2,3},{3,0},{4,5},{5,6},{6,7},{7,4},{8,9},{9,10},{10,1... | collective-permute-start | bytes 1572872 | tf_op jit(solution)/shard_map/ppermute | solution.py:589
  261.1 11.2 %all-to-all-start.5 = ((f32[8,72,128]{2,1,0:T(8,128)}), f32[8,72,128]{2,1,0:T(8,128)S(1)}, u32[]{:S(2)}, u32[]{:S(2)}) async-start(f32[8,72,128]{2,1,0:T(8,128)} %broadcast_in_dim.80), calls=%async_computation.5 | async-start | bytes 589824 | tf_op jit(solution)/shard_map/all_to_all | solution.py:541
  (28 other events, 460.4 us)
